TPU v7x, 256 devices: a whole 4x4x8 slice. The times are simulated.
256 devices in a mesh: dp: 8 (over x, y_hi), row: 4 (over y_lo, core), col: 8 (over z).
Axes of the slice: x: 4, y: 4 (y_hi: 2, y_lo: 2; y = y_hi * 2 + y_lo), z: 8, core: 2. Of those that a mesh axis runs over, the one named last changes fastest.
Arguments:
- teacher_in: bfloat16 [8, 128, 256, 384], P('dp', 'row', 'col'), may hold values from -6 to 6
- student_in: bfloat16 [8, 128, 256, 384], P('dp', 'row', 'col'), may hold values from -6 to 6
- cotangent: bfloat16 [8, 128, 256, 384], P('dp', 'row', 'col'), may hold values from -6 to 6
- kernels: bfloat16 [2, 49, 384], replicated, may hold values from -0.875 to 0.875
- norm_gains: bfloat16 [2, 2, 384], replicated, may hold values from 0.25 to 1.75
- biases: bfloat16 [2, 3, 384], replicated, may hold values from -3 to 3
- weight_in: bfloat16 [2, 384, 1536], P(None, None, 'dp'), may hold values from -0.3125 to 0.3125
- bias_in: bfloat16 [2, 1536], P(None, 'dp'), may hold values from -3 to 3
- weight_out: bfloat16 [2, 1536, 384], P(None, 'dp'), may hold values from -0.15625 to 0.15625
Outputs:
- teacher_out: float32 [8, 128, 256, 384], P('dp', 'row', 'col')
- student_out: float32 [8, 128, 256, 384], P('dp', 'row', 'col')
- input_grad: float32 [8, 128, 256, 384], P('dp', 'row', 'col')
- grad_weight_in: float32 [384, 1536], P(None, 'dp')
- grad_bias_in: float32 [1536], P('dp')
- grad_weight_out: float32 [1536, 384], P('dp')
- grad_kernel: float32 [49, 384], replicated
- grad_gains: float32 [2, 384], replicated
- grad_biases: float32 [3, 384], replicated
All inputs are finite; a program needn't handle non-finite values.
Results may differ from a plain program's by a relative error of at most 0.0057.
Values may be sent and summed in bfloat16 or wider, within the bound.
No kernel may reach another device: no remote copies, remote signals or barrier semaphores. Data moves between devices by JAX's collectives and lax.ppermute only.
A program may use at most 128 MiB of HBM per device.

v0:
```python
import jax
import jax.numpy as jnp
from jax import lax
from jax.sharding import PartitionSpec as P

KERNEL = 7
EPSILON = 1e-06
ROOT_HALF = 0.7071067811865476
INV_ROOT_TWO_PI = 0.3989422804014327


def with_halo(value, sides, width):
    for axis, dim in sides:
        peers, length = (lax.axis_size(axis), value.shape[dim])
        up = [(i, (i + 1) % peers) for i in range(peers - 1)]
        down = [(j, i) for i, j in up]
        last = lax.slice_in_dim(value, length - width, length, axis=dim)
        leading = lax.slice_in_dim(value, 0, width, axis=dim)
        before = lax.ppermute(last, axis, up)
        after = lax.ppermute(leading, axis, down)
        value = jnp.concatenate([before, value, after], axis=dim)
    return value


def gelu_value(before):
    return before * 0.5 * (1.0 + lax.erf(before * ROOT_HALF))


def gelu_slope(before):
    return 0.5 * (1.0 + lax.erf(before * ROOT_HALF)) + before * INV_ROOT_TWO_PI * jnp.exp(
        -0.5 * before * before
    )


def depthwise(padded, kernel, height, breadth):
    running = jnp.zeros((padded.shape[0], height, breadth, padded.shape[3]), jnp.float32)
    for position in range(KERNEL * KERNEL):
        vertical = position // KERNEL
        lateral = position % KERNEL
        window = padded[:, vertical : vertical + height, lateral : lateral + breadth, :]
        running = running + window.astype(jnp.float32) * kernel[position].astype(jnp.float32)
    return running


def forward(padded, inputs, kernel, norm_gains, biases, weight_in, bias_in, weight_out):
    height, breadth, channels = (inputs.shape[1], inputs.shape[2], inputs.shape[3])
    convolved = depthwise(padded, kernel, height, breadth) + biases[0].astype(jnp.float32)
    centered = convolved - jnp.mean(convolved, axis=-1, keepdims=True)
    inverse = lax.rsqrt(jnp.mean(centered * centered, axis=-1, keepdims=True) + EPSILON)
    scaled = centered * inverse
    normed = (scaled * norm_gains[0].astype(jnp.float32) + biases[1].astype(jnp.float32)).astype(
        jnp.bfloat16
    )
    normed = normed.reshape(-1, channels)
    before = jnp.dot(normed, weight_in, preferred_element_type=jnp.float32) + bias_in.astype(
        jnp.float32
    )
    hidden = gelu_value(before).astype(jnp.bfloat16)
    branch = jnp.dot(hidden, weight_out, preferred_element_type=jnp.float32) + biases[2].astype(
        jnp.float32
    )
    output = inputs.astype(jnp.float32) + norm_gains[1].astype(jnp.float32) * branch.reshape(
        inputs.shape
    )
    return (output, (scaled, inverse, normed, before, hidden, branch))


def backward(cotangent, padded, stored, norm_gains, weight_in, weight_out):
    scaled, inverse, normed, before, hidden, branch = stored
    height, breadth, channels = (cotangent.shape[1], cotangent.shape[2], cotangent.shape[3])
    flat_grad = cotangent.astype(jnp.float32).reshape(-1, channels)
    grad_gamma = jnp.sum(flat_grad * branch, axis=0)
    branch_grad = (flat_grad * norm_gains[1].astype(jnp.float32)).astype(jnp.bfloat16)
    branch_grad = lax.optimization_barrier(branch_grad)
    grad_out_bias = jnp.sum(branch_grad.astype(jnp.float32), axis=0)
    grad_weight_out = jnp.dot(hidden.T, branch_grad, preferred_element_type=jnp.float32)
    hidden_grad = jnp.dot(branch_grad, weight_out.T, preferred_element_type=jnp.float32)
    before_grad = (hidden_grad * gelu_slope(before)).astype(jnp.bfloat16)
    before_grad = lax.optimization_barrier(before_grad)
    grad_bias_in = jnp.sum(before_grad.astype(jnp.float32), axis=0)
    grad_weight_in = jnp.dot(normed.T, before_grad, preferred_element_type=jnp.float32)
    normed_grad = jnp.dot(before_grad, weight_in.T, preferred_element_type=jnp.float32).reshape(
        scaled.shape
    )
    grad_norm_gain = jnp.sum(normed_grad * scaled, axis=(0, 1, 2))
    grad_norm_bias = jnp.sum(normed_grad, axis=(0, 1, 2))
    scaled_grad = normed_grad * norm_gains[0].astype(jnp.float32)
    conv_grad = inverse * (
        scaled_grad
        - jnp.mean(scaled_grad, axis=-1, keepdims=True)
        - scaled * jnp.mean(scaled_grad * scaled, axis=-1, keepdims=True)
    )
    conv_grad = lax.optimization_barrier(conv_grad.astype(jnp.bfloat16))
    conv_wide = conv_grad.astype(jnp.float32)
    grad_conv_bias = jnp.sum(conv_wide, axis=(0, 1, 2))
    tap_sums = []
    for position in range(KERNEL * KERNEL):
        vertical = position // KERNEL
        lateral = position % KERNEL
        window = padded[:, vertical : vertical + height, lateral : lateral + breadth, :].astype(
            jnp.float32
        )
        tap_sums.append(jnp.sum(window * conv_wide, axis=(0, 1, 2)))
    grad_kernel = jnp.stack(tap_sums)
    large_grads = (grad_weight_in, grad_bias_in, grad_weight_out)
    minor_grads = (
        grad_kernel,
        jnp.stack([grad_norm_gain, grad_gamma]),
        jnp.stack([grad_conv_bias, grad_norm_bias, grad_out_bias]),
    )
    return (conv_grad, large_grads, minor_grads)


def input_gradient(cotangent, padded_grad, kernel):
    height, breadth = (cotangent.shape[1], cotangent.shape[2])
    flipped = depthwise(padded_grad, kernel[::-1], height, breadth)
    return cotangent.astype(jnp.float32) + flipped


def on_device(
    teacher_in, student_in, cotangent, kernels, norm_gains, biases, weight_in, bias_in, weight_out
):
    margin = KERNEL // 2
    full_in, full_bias, full_out = (
        lax.all_gather(weight_in, "dp", axis=2, tiled=True),
        lax.all_gather(bias_in, "dp", axis=1, tiled=True),
        lax.all_gather(weight_out, "dp", axis=1, tiled=True),
    )
    teacher_pad = with_halo(teacher_in, (("row", 1), ("col", 2)), margin)
    student_pad = with_halo(student_in, (("row", 1), ("col", 2)), margin)
    teacher_res, unused = forward(
        teacher_pad,
        teacher_in,
        kernels[0],
        norm_gains[0],
        biases[0],
        full_in[0],
        full_bias[0],
        full_out[0],
    )
    student_res, stored = forward(
        student_pad,
        student_in,
        kernels[1],
        norm_gains[1],
        biases[1],
        full_in[1],
        full_bias[1],
        full_out[1],
    )
    conv_grad, large_grads, minor_grads = backward(
        cotangent, student_pad, stored, norm_gains[1], full_in[1], full_out[1]
    )
    grad_pad = with_halo(conv_grad, (("row", 1), ("col", 2)), margin)
    in_grad = input_gradient(cotangent, grad_pad, kernels[1])
    minor_sums = lax.psum((minor_grads[0], minor_grads[1], minor_grads[2]), ("dp", "row", "col"))
    owned = (
        lax.psum_scatter(large_grads[0], "dp", scatter_dimension=1, tiled=True),
        lax.psum_scatter(large_grads[1], "dp", scatter_dimension=0, tiled=True),
        lax.psum_scatter(large_grads[2], "dp", scatter_dimension=0, tiled=True),
    )
    shares = lax.psum((owned[0], owned[1], owned[2]), ("row", "col"))
    tokens = (
        teacher_in.shape[0]
        * teacher_in.shape[1]
        * teacher_in.shape[2]
        * lax.axis_size("dp")
        * lax.axis_size("row")
        * lax.axis_size("col")
    )
    factor = float(tokens) ** (-0.5)
    return (
        teacher_res,
        student_res,
        in_grad,
        shares[0] * factor,
        shares[1] * factor,
        shares[2] * factor,
        minor_sums[0] * factor,
        minor_sums[1] * factor,
        minor_sums[2] * factor,
    )


def solution(mesh):
    placed = (
        P("dp", "row", "col", None),
        P("dp", "row", "col", None),
        P("dp", "row", "col", None),
        P(),
        P(),
        P(),
        P(None, None, "dp"),
        P(None, "dp"),
        P(None, "dp", None),
    )
    return jax.shard_map(
        on_device,
        mesh=mesh,
        in_specs=placed,
        out_specs=(
            P("dp", "row", "col", None),
            P("dp", "row", "col", None),
            P("dp", "row", "col", None),
            P(None, "dp"),
            P("dp"),
            P("dp", None),
            P(),
            P(),
            P(),
        ),
        check_vma=False,
    )
```

profile of v0, /device:TPU:1, one launch (start us, length us, event | category | flops | bytes accessed | tf_op | source)
XLA Modules:
  0.0 829.3 jit_solution(6039890744320597389)
XLA Ops:
  8.9 4.6 collective-permute-start
  13.5 1.9 collective-permute-start.1
  16.4 3.6 collective-permute-start.4
  20.0 1.9 collective-permute-start.5
  26.0 1.5 convert_reduce_fusion.55
  27.7 1.4 convert_reduce_fusion.3
  29.1 1.4 convert_reduce_fusion.56
  30.5 19.7 %all-gather = bf16[8,192,2]{1,2,0:T(2,128)(2,1)S(1)} all-gather(bf16[1,192,2]{1,2,0:T(2,128)(2,1)} %bitcast.59), channel_id=1, replica_groups=mesh['dp'=8,'row'=4,'col'=8] {'dp'}, dimensions={0}, use_global_device_ids=true | all-gather | bytes 6912 | tf_op jit(solution)/shard_map/all_gather | solution.py:126
  52.3 3.5 collective-permute-start.2
  55.8 1.3 collective-permute-start.3
  57.7 4.2 collective-permute-start.6
  62.0 1.5 collective-permute-start.7
  63.5 15.8 %fusion.250 = (f32[32,32]{1,0:T(8,128)S(1)}, f32[1,32,32,384]{3,2,1,0:T(8,128)S(1)}) fusion(f32[384]{0:T(512)S(1)} %get-tuple-element.174, f32[384]{0:T(512)S(1)} %get-tuple-element.117, bf16[1,38,3,384]{3,2,1,0:T(4,128)(2,1)S(1)} %collective-permute-done.3, bf16[1,38,32,384]{3,2,1,0:T(8,128)(2,1)S(1)} %get-tuple-element.218, ...), kind=kLoop, calls=%fused_computation.649 | loop fusion | flops 107740160 | bytes 8267776 | tf_op jit(solution)/shard_map/reduce_sum | solution.py:48
  80.0 16.4 %fusion.248 = (f32[32,32]{1,0:T(8,128)S(1)}, f32[1,32,32,384]{3,2,1,0:T(8,128)S(1)}) fusion(f32[384]{0:T(512)S(1)} %get-tuple-element.171, f32[384]{0:T(512)S(1)} %get-tuple-element.146, bf16[1,38,3,384]{3,2,1,0:T(4,128)(2,1)S(1)} %collective-permute-done.7, bf16[1,38,32,384]{3,2,1,0:T(8,128)(2,1)S(1)} %get-tuple-element.214, ...), kind=kLoop, calls=%fused_computation.648 | loop fusion | flops 107740160 | bytes 8267776 | tf_op jit(solution)/shard_map/reduce_sum | solution.py:48
  96.9 1.5 add_convert_fusion
  98.4 6.7 multiply_convert_fusion
  105.1 33.4 %all-gather.6.cloned.1.call-done = bf16[2,1536,384]{2,1,0:T(8,128)(2,1)} async-done(((bf16[2,192,384]{2,1,0:T(8,128)(2,1)}), bf16[2,1536,384]{2,1,0:T(8,128)(2,1)}) %all-gather.6.cloned.1.call-update) | async-done | bytes 2359312 | tf_op jit(solution)/shard_map/all_gather | solution.py:127
  138.5 5.4 fusion.153
  143.9 4.3 fusion.4
  148.2 1.9 fusion.247
  150.1 1.1 copy-done.6
  152.0 2.1 multiply_convert_fusion.2
  155.3 2.6 fusion.146
  158.0 3.2 fusion.150
  161.4 2.6 fusion.147
  164.1 3.1 fusion.151
  167.4 3.6 fusion.149
  171.1 4.4 stack.220
  175.5 5.2 fusion.258
  181.8 5.1 fusion.257
  189.1 4.3 collective-permute-start.8
  193.5 2.1 collective-permute-start.9
  195.5 2.4 convert_reduce_fusion.1
  197.9 19.3 %all-reduce = f32[1536]{0:T(1024)S(1)} all-reduce(f32[1536]{0:T(1024)S(1)} %convert_reduce_fusion.1), channel_id=3, replica_groups=mesh['dp'=8,'row'=4,'col'=8] {'dp'}, use_global_device_ids=true, to_apply=%region_9.0.clone | all-reduce | flops 1536 | bytes 12288
  217.3 54.5 %psum.43 = f32[192]{0:T(256)S(1)} all-reduce(f32[192]{0:T(256)S(1)} %dynamic-slice.1), channel_id=1, replica_groups=mesh['dp'=8,'row'=4,'col'=8] {'row','col'}, use_global_device_ids=true, to_apply=%region_10.0 | all-reduce | flops 192 | bytes 1536 | tf_op jit(solution)/shard_map/psum | solution.py:162
  271.8 77.7 %all-reduce.1 = (f32[2,384]{1,0:T(2,128)S(1)}, f32[3,384]{1,0:T(4,128)S(1)}) all-reduce(f32[2,384]{1,0:T(2,128)S(1)} %pad_maximum_fusion.11, f32[3,384]{1,0:T(4,128)S(1)} %pad_maximum_fusion.10), channel_id=1, replica_groups=mesh['dp'=8,'row'=4,'col'=8] {'dp','row','col'}, use_global_device_ids=true, to_apply=%region_65.0 | all-reduce | flops 1920 | bytes 15360 | tf_op jit(solution)/shard_map/psum | solution.py:156
  350.7 6.3 convolution_add_fusion.1
  357.0 2.8 convert_add_fusion.1
  360.5 2.3 collective-permute-start.10
  362.8 1.3 collective-permute-start.11
  364.1 56.6 %all-reduce.6.cloned.1.call-done = f32[49,384]{1,0:T(8,128)} async-done(((f32[49,384]{1,0:T(8,128)}), f32[49,384]{1,0:T(8,128)}) %all-reduce.6.cloned.1.call-update) | async-done | bytes 75280 | tf_op jit(solution)/shard_map/psum | solution.py:156
  420.7 1.5 broadcast_multiply_fusion.2
  423.0 79.1 %reduce-scatter.5.cloned.1.call-done = f32[192,384]{1,0:T(8,128)} async-done(((f32[1536,384]{1,0:T(8,128)}), f32[192,384]{1,0:T(8,128)}) %reduce-scatter.5.cloned.1.call-update) | async-done | bytes 294928 | tf_op jit(solution)/shard_map/reduce_scatter | solution.py:160
  502.1 85.7 %reduce-scatter.3.cloned.1.call-done = f32[384,192]{0,1:T(8,128)} async-done(((f32[384,1536]{0,1:T(8,128)}), f32[384,192]{0,1:T(8,128)}) %reduce-scatter.3.cloned.1.call-update) | async-done | bytes 294928 | tf_op jit(solution)/shard_map/reduce_scatter | solution.py:158
  587.9 17.0 %convert_add_fusion.2 = f32[1,32,32,384]{3,2,1,0:T(8,128)} fusion(bf16[1,32,32,384]{3,2,1,0:T(8,128)(2,1)} %param.11, bf16[1,32,32,384]{3,2,1,0:T(8,128)(2,1)S(1)} %multiply_convert_fusion.2, bf16[1,3,32,384]{3,2,1,0:T(8,128)(2,1)S(1)} %collective-permute-done.9, bf16[1,3,32,384]{3,2,1,0:T(8,128)(2,1)S(1)} %collective-permute-done.8, ...), kind=kLoop, calls=%fused_computation.342 | loop fusion | flops 60555264 | bytes 36398592 | tf_op jit(solution)/shard_map/add | solution.py:117
  604.9 214.2 %all-reduce.8.cloned.1.call-done = (f32[384,192]{0,1:T(8,128)}, f32[192,384]{1,0:T(8,128)}) async-done(((f32[384,192]{0,1:T(8,128)}, f32[192,384]{1,0:T(8,128)}), (f32[384,192]{0,1:T(8,128)}, f32[192,384]{1,0:T(8,128)})) %all-reduce.8.cloned.1.call-update) | async-done | bytes 589840 | tf_op jit(solution)/shard_map/psum | solution.py:162
  819.0 1.7 broadcast_multiply_fusion
  820.7 1.7 broadcast_multiply_fusion.1
  (248 shorter events, 17.5 us)
Async XLA Ops:
  7.2 91.2 %all-gather.4.cloned.1.call-start = ((), (), s32[]{:S(2)}) async-start(), calls=%async_computation.2 | async-start | bytes 2654208 | tf_op jit(solution)/shard_map/all_gather | solution.py:125
  7.9 130.6 %all-gather.6.cloned.1.call-start = ((), (), s32[]{:S(2)}) async-start(), calls=%async_computation.3 | async-start | bytes 2654208 | tf_op jit(solution)/shard_map/all_gather | solution.py:127
  8.9 42.8 %collective-permute-start = (bf16[1,3,32,384]{3,2,1,0:T(8,128)(2,1)S(1)}, bf16[1,3,32,384]{3,2,1,0:T(8,128)(2,1)S(1)}, u32[]{:S(2)}, u32[]{:S(2)}) collective-permute-start(bf16[1,3,32,384]{3,2,1,0:T(8,128)(2,1)S(1)} %get-tuple-element.210), channel_id=1, source_target_pairs={{0,8},{8,16},{16,24},{1,9},{9,17},{17,25},{2,10},{10,18},{18,26},{... | collective-permute-start | bytes 221192 | tf_op jit(solution)/shard_map/ppermute | solution.py:19
  13.5 38.6 %collective-permute-start.1 = (bf16[1,3,32,384]{3,2,1,0:T(8,128)(2,1)S(1)}, bf16[1,3,32,384]{3,2,1,0:T(8,128)(2,1)S(1)}, u32[]{:S(2)}, u32[]{:S(2)}) collective-permute-start(bf16[1,3,32,384]{3,2,1,0:T(8,128)(2,1)S(1)} %get-tuple-element.209), channel_id=1, source_target_pairs={{8,0},{16,8},{24,16},{9,1},{17,9},{25,17},{10,2},{18,10},{26,18},{... | collective-permute-start | bytes 221192 | tf_op jit(solution)/shard_map/ppermute | solution.py:20
  16.4 40.7 %collective-permute-start.4 = (bf16[1,3,32,384]{3,2,1,0:T(8,128)(2,1)S(1)}, bf16[1,3,32,384]{3,2,1,0:T(8,128)(2,1)S(1)}, u32[]{:S(2)}, u32[]{:S(2)}) collective-permute-start(bf16[1,3,32,384]{3,2,1,0:T(8,128)(2,1)S(1)} %get-tuple-element.205), channel_id=1, source_target_pairs={{0,8},{8,16},{16,24},{1,9},{9,17},{17,25},{2,10},{10,18},{18,26},{... | collective-permute-start | bytes 221192 | tf_op jit(solution)/shard_map/ppermute | solution.py:19
  20.0 37.5 %collective-permute-start.5 = (bf16[1,3,32,384]{3,2,1,0:T(8,128)(2,1)S(1)}, bf16[1,3,32,384]{3,2,1,0:T(8,128)(2,1)S(1)}, u32[]{:S(2)}, u32[]{:S(2)}) collective-permute-start(bf16[1,3,32,384]{3,2,1,0:T(8,128)(2,1)S(1)} %get-tuple-element.204), channel_id=1, source_target_pairs={{8,0},{16,8},{24,16},{9,1},{17,9},{25,17},{10,2},{18,10},{26,18},{... | collective-permute-start | bytes 221192 | tf_op jit(solution)/shard_map/ppermute | solution.py:20
  22.0 398.7 %all-reduce.6.cloned.1.call-start = ((), (), s32[]{:S(2)}) async-start(), calls=%async_computation.6 | async-start | bytes 172032 | tf_op jit(solution)/shard_map/psum | solution.py:156
  25.9 53.8 %copy-start.19 = (f32[384]{0:T(512)}, f32[384]{0:T(512)S(1)}, u32[]{:S(2)}) copy-start(f32[384]{0:T(512)S(1)} %get-tuple-element.90) | copy-start | bytes 4612
  25.9 53.8 %copy-start.20 = (f32[384]{0:T(512)}, f32[384]{0:T(512)S(1)}, u32[]{:S(2)}) copy-start(f32[384]{0:T(512)S(1)} %get-tuple-element.91) | copy-start | bytes 4612
  25.9 53.8 %copy-start.21 = (f32[384]{0:T(512)}, f32[384]{0:T(512)S(1)}, u32[]{:S(2)}) copy-start(f32[384]{0:T(512)S(1)} %get-tuple-element.92) | copy-start | bytes 4612
  25.9 53.8 %copy-start.22 = (f32[384]{0:T(512)}, f32[384]{0:T(512)S(1)}, u32[]{:S(2)}) copy-start(f32[384]{0:T(512)S(1)} %get-tuple-element.93) | copy-start | bytes 4612
  25.9 53.8 %copy-start.23 = (f32[384]{0:T(512)}, f32[384]{0:T(512)S(1)}, u32[]{:S(2)}) copy-start(f32[384]{0:T(512)S(1)} %get-tuple-element.94) | copy-start | bytes 4612
  25.9 53.8 %copy-start.24 = (f32[384]{0:T(512)}, f32[384]{0:T(512)S(1)}, u32[]{:S(2)}) copy-start(f32[384]{0:T(512)S(1)} %get-tuple-element.95) | copy-start | bytes 4612
  25.9 53.8 %copy-start.25 = (f32[384]{0:T(512)}, f32[384]{0:T(512)S(1)}, u32[]{:S(2)}) copy-start(f32[384]{0:T(512)S(1)} %get-tuple-element.96) | copy-start | bytes 4612
  25.9 53.8 %copy-start.26 = (f32[384]{0:T(512)}, f32[384]{0:T(512)S(1)}, u32[]{:S(2)}) copy-start(f32[384]{0:T(512)S(1)} %get-tuple-element.97) | copy-start | bytes 4612
  25.9 53.8 %copy-start.27 = (f32[384]{0:T(512)}, f32[384]{0:T(512)S(1)}, u32[]{:S(2)}) copy-start(f32[384]{0:T(512)S(1)} %get-tuple-element.98) | copy-start | bytes 4612
  25.9 53.8 %copy-start.28 = (f32[384]{0:T(512)}, f32[384]{0:T(512)S(1)}, u32[]{:S(2)}) copy-start(f32[384]{0:T(512)S(1)} %get-tuple-element.99) | copy-start | bytes 4612
  26.0 53.8 %copy-start.29 = (f32[384]{0:T(512)}, f32[384]{0:T(512)S(1)}, u32[]{:S(2)}) copy-start(f32[384]{0:T(512)S(1)} %get-tuple-element.100) | copy-start | bytes 4612
  26.0 53.8 %copy-start.30 = (f32[384]{0:T(512)}, f32[384]{0:T(512)S(1)}, u32[]{:S(2)}) copy-start(f32[384]{0:T(512)S(1)} %get-tuple-element.101) | copy-start | bytes 4612
  26.0 53.8 %copy-start.31 = (f32[384]{0:T(512)}, f32[384]{0:T(512)S(1)}, u32[]{:S(2)}) copy-start(f32[384]{0:T(512)S(1)} %get-tuple-element.102) | copy-start | bytes 4612
  26.0 53.8 %copy-start.32 = (f32[384]{0:T(512)}, f32[384]{0:T(512)S(1)}, u32[]{:S(2)}) copy-start(f32[384]{0:T(512)S(1)} %get-tuple-element.103) | copy-start | bytes 4612
  26.0 53.8 %copy-start.33 = (f32[384]{0:T(512)}, f32[384]{0:T(512)S(1)}, u32[]{:S(2)}) copy-start(f32[384]{0:T(512)S(1)} %get-tuple-element.104) | copy-start | bytes 4612
  26.0 53.8 %copy-start.34 = (f32[384]{0:T(512)}, f32[384]{0:T(512)S(1)}, u32[]{:S(2)}) copy-start(f32[384]{0:T(512)S(1)} %get-tuple-element.105) | copy-start | bytes 4612
  26.0 53.8 %copy-start.35 = (f32[384]{0:T(512)}, f32[384]{0:T(512)S(1)}, u32[]{:S(2)}) copy-start(f32[384]{0:T(512)S(1)} %get-tuple-element.106) | copy-start | bytes 4612
  26.0 53.8 %copy-start.36 = (f32[384]{0:T(512)}, f32[384]{0:T(512)S(1)}, u32[]{:S(2)}) copy-start(f32[384]{0:T(512)S(1)} %get-tuple-element.107) | copy-start | bytes 4612
  27.6 52.3 %copy-start.42 = (f32[384]{0:T(512)}, f32[384]{0:T(512)S(1)}, u32[]{:S(2)}) copy-start(f32[384]{0:T(512)S(1)} %get-tuple-element.75) | copy-start | bytes 4612
  27.6 52.3 %copy-start.43 = (f32[384]{0:T(512)}, f32[384]{0:T(512)S(1)}, u32[]{:S(2)}) copy-start(f32[384]{0:T(512)S(1)} %get-tuple-element.76) | copy-start | bytes 4612
  27.6 52.3 %copy-start.44 = (f32[384]{0:T(512)}, f32[384]{0:T(512)S(1)}, u32[]{:S(2)}) copy-start(f32[384]{0:T(512)S(1)} %get-tuple-element.77) | copy-start | bytes 4612
  27.6 52.3 %copy-start.45 = (f32[384]{0:T(512)}, f32[384]{0:T(512)S(1)}, u32[]{:S(2)}) copy-start(f32[384]{0:T(512)S(1)} %get-tuple-element.78) | copy-start | bytes 4612
  27.6 52.3 %copy-start.46 = (f32[384]{0:T(512)}, f32[384]{0:T(512)S(1)}, u32[]{:S(2)}) copy-start(f32[384]{0:T(512)S(1)} %get-tuple-element.79) | copy-start | bytes 4612
  27.6 52.3 %copy-start.47 = (f32[384]{0:T(512)}, f32[384]{0:T(512)S(1)}, u32[]{:S(2)}) copy-start(f32[384]{0:T(512)S(1)} %get-tuple-element.80) | copy-start | bytes 4612
  27.7 52.3 %copy-start.48 = (f32[384]{0:T(512)}, f32[384]{0:T(512)S(1)}, u32[]{:S(2)}) copy-start(f32[384]{0:T(512)S(1)} %get-tuple-element.81) | copy-start | bytes 4612
  27.7 52.3 %copy-start.49 = (f32[384]{0:T(512)}, f32[384]{0:T(512)S(1)}, u32[]{:S(2)}) copy-start(f32[384]{0:T(512)S(1)} %get-tuple-element.82) | copy-start | bytes 4612
  27.7 52.3 %copy-start.50 = (f32[384]{0:T(512)}, f32[384]{0:T(512)S(1)}, u32[]{:S(2)}) copy-start(f32[384]{0:T(512)S(1)} %get-tuple-element.83) | copy-start | bytes 4612
  52.3 11.2 %collective-permute-start.2 = (bf16[1,38,3,384]{3,2,1,0:T(4,128)(2,1)S(1)}, bf16[1,38,3,384]{3,2,1,0:T(4,128)(2,1)S(1)}, u32[]{:S(2)}, u32[]{:S(2)}) collective-permute-start(bf16[1,38,3,384]{3,2,1,0:T(4,128)(2,1)S(1)} %get-tuple-element.194), channel_id=1, source_target_pairs={{0,1},{1,2},{2,3},{3,4},{4,5},{5,6},{6,7},{8,9},{9,10},{10,11},{11... | collective-permute-start | bytes 262664 | tf_op jit(solution)/shard_map/ppermute | solution.py:19
  55.8 7.7 collective-permute-start.3
  57.7 21.9 %collective-permute-start.6 = (bf16[1,38,3,384]{3,2,1,0:T(4,128)(2,1)S(1)}, bf16[1,38,3,384]{3,2,1,0:T(4,128)(2,1)S(1)}, u32[]{:S(2)}, u32[]{:S(2)}) collective-permute-start(bf16[1,38,3,384]{3,2,1,0:T(4,128)(2,1)S(1)} %get-tuple-element.192), channel_id=1, source_target_pairs={{0,1},{1,2},{2,3},{3,4},{4,5},{5,6},{6,7},{8,9},{9,10},{10,11},{11... | collective-permute-start | bytes 262664 | tf_op jit(solution)/shard_map/ppermute | solution.py:19
  62.0 17.7 %collective-permute-start.7 = (bf16[1,38,3,384]{3,2,1,0:T(4,128)(2,1)S(1)}, bf16[1,38,3,384]{3,2,1,0:T(4,128)(2,1)S(1)}, u32[]{:S(2)}, u32[]{:S(2)}) collective-permute-start(bf16[1,38,3,384]{3,2,1,0:T(4,128)(2,1)S(1)} %get-tuple-element.193), channel_id=1, source_target_pairs={{1,0},{2,1},{3,2},{4,3},{5,4},{6,5},{7,6},{9,8},{10,9},{11,10},{12... | collective-permute-start | bytes 262664 | tf_op jit(solution)/shard_map/ppermute | solution.py:20
  175.5 326.6 %reduce-scatter.5.cloned.1.call-start = ((), (), s32[]{:S(2)}) async-start(), calls=%async_computation.5 | async-start | bytes 2654208 | tf_op jit(solution)/shard_map/reduce_scatter | solution.py:160
  180.7 407.1 %reduce-scatter.3.cloned.1.call-start = ((), (), s32[]{:S(2)}) async-start(), calls=%async_computation.4 | async-start | bytes 2654208 | tf_op jit(solution)/shard_map/reduce_scatter | solution.py:158
  187.0 632.0 %all-reduce.8.cloned.1.call-start = ((), (), s32[]{:S(2)}) async-start(), calls=%async_computation.7 | async-start | bytes 1179648 | tf_op jit(solution)/shard_map/psum | solution.py:162
  189.1 171.2 %collective-permute-start.8 = (bf16[1,3,32,384]{3,2,1,0:T(8,128)(2,1)S(1)}, bf16[1,3,32,384]{3,2,1,0:T(8,128)(2,1)S(1)}, u32[]{:S(2)}, u32[]{:S(2)}) collective-permute-start(bf16[1,3,32,384]{3,2,1,0:T(8,128)(2,1)S(1)} %get-tuple-element.199), channel_id=1, source_target_pairs={{0,8},{8,16},{16,24},{1,9},{9,17},{17,25},{2,10},{10,18},{18,26},{... | collective-permute-start | bytes 221192 | tf_op jit(solution)/shard_map/ppermute | solution.py:19
  193.4 157.2 %copy-start.13 = (bf16[1,32,32,384]{3,2,1,0:T(8,128)(2,1)S(1)}, bf16[1,32,32,384]{3,2,1,0:T(8,128)(2,1)}, u32[]{:S(2)}) copy-start(bf16[1,32,32,384]{3,2,1,0:T(8,128)(2,1)} %get-tuple-element.224) | copy-start | bytes 2359300
  193.5 157.2 %copy-start.57 = (f32[1536]{0:T(1024)S(1)}, f32[1536]{0:T(1024)}, u32[]{:S(2)}) copy-start(f32[1536]{0:T(1024)} %get-tuple-element.169) | copy-start | bytes 18436
  193.5 157.2 %copy-start.59 = (f32[384]{0:T(512)S(1)}, f32[384]{0:T(512)}, u32[]{:S(2)}) copy-start(f32[384]{0:T(512)} %get-tuple-element.172) | copy-start | bytes 4612
  193.5 166.9 %collective-permute-start.9 = (bf16[1,3,32,384]{3,2,1,0:T(8,128)(2,1)S(1)}, bf16[1,3,32,384]{3,2,1,0:T(8,128)(2,1)S(1)}, u32[]{:S(2)}, u32[]{:S(2)}) collective-permute-start(bf16[1,3,32,384]{3,2,1,0:T(8,128)(2,1)S(1)} %get-tuple-element.200), channel_id=1, source_target_pairs={{8,0},{16,8},{24,16},{9,1},{17,9},{25,17},{10,2},{18,10},{26,18},{... | collective-permute-start | bytes 221192 | tf_op jit(solution)/shard_map/ppermute | solution.py:20
  360.5 61.8 %collective-permute-start.10 = (bf16[1,38,3,384]{3,2,1,0:T(4,128)(2,1)S(1)}, bf16[1,38,3,384]{3,2,1,0:T(4,128)(2,1)S(1)}, u32[]{:S(2)}, u32[]{:S(2)}) collective-permute-start(bf16[1,38,3,384]{3,2,1,0:T(4,128)(2,1)S(1)} %get-tuple-element.190), channel_id=1, source_target_pairs={{0,1},{1,2},{2,3},{3,4},{4,5},{5,6},{6,7},{8,9},{9,10},{10,11},{11... | collective-permute-start | bytes 262664 | tf_op jit(solution)/shard_map/ppermute | solution.py:19
  362.8 59.5 %collective-permute-start.11 = (bf16[1,38,3,384]{3,2,1,0:T(4,128)(2,1)S(1)}, bf16[1,38,3,384]{3,2,1,0:T(4,128)(2,1)S(1)}, u32[]{:S(2)}, u32[]{:S(2)}) collective-permute-start(bf16[1,38,3,384]{3,2,1,0:T(4,128)(2,1)S(1)} %get-tuple-element.191), channel_id=1, source_target_pairs={{1,0},{2,1},{3,2},{4,3},{5,4},{6,5},{7,6},{9,8},{10,9},{11,10},{12... | collective-permute-start | bytes 262664 | tf_op jit(solution)/shard_map/ppermute | solution.py:20
  (35 other events, 782.8 us)
Sparse Core Ops, SparseCore 0:
  10.6 64.3 all-gather.3
  77.6 60.8 all-gather.5
  175.6 245.0 all-reduce.5
  424.7 77.4 reduce-scatter.4
  506.1 81.7 reduce-scatter.2
  590.4 228.6 all-reduce.7
where the time goes:
time: 831 us; the launch traced here: 829 us
  waiting for transfers between devices  470 us (57%)
  blocking collectives  171 us (21%)
  other arithmetic  92.2 us (11%)
  matrix products  34.8 us (4%)
  starting transfers between devices  32.8 us (4%)
  between operations  16.4 us (2%)
  local copies, waits for them, and re-layouts  12.1 us (1%)
    psum x1, waiting for transfers between devices, on_device(): shares = lax.psum((owned[0], owned[1], owned[2]), ('row', 'col'))  214 us
    reduce_scatter x1, waiting for transfers between devices, on_device(): lax.psum_scatter(large_grads[0], 'dp', scatter_dimension=1, tiled=True)  85.7 us
    reduce_scatter x1, waiting for transfers between devices, on_device(): lax.psum_scatter(large_grads[2], 'dp', scatter_dimension=0, tiled=True)  79.1 us
    psum x1, blocking collectives, on_device(): lax.psum((minor_grads[0], minor_grads[1], minor_grads[2]), ('dp', 'row',...  77.7 us
    psum x1, waiting for transfers between devices, on_device(): lax.psum((minor_grads[0], minor_grads[1], minor_grads[2]), ('dp', 'row',...  56.6 us
    psum x1, blocking collectives, on_device(): shares = lax.psum((owned[0], owned[1], owned[2]), ('row', 'col'))  54.5 us
    all_gather x1, waiting for transfers between devices, on_device(): lax.all_gather(weight_out, 'dp', axis=1, tiled=True)  33.4 us
    reduce_sum x2, other arithmetic, forward(): centered = convolved - jnp.mean(convolved, axis=-1, keepdims=True)  32.2 us
  transfers between devices with their start and end apart: 18, of which 5 were waited for; matrix products, arithmetic and copies ran while one was open for 12% of the time, Pallas kernels for 0%

commit v1 on v0

--- a/solution.py
+++ b/solution.py
@@ -153,7 +153,9 @@
     )
     grad_pad = with_halo(conv_grad, (("row", 1), ("col", 2)), margin)
     in_grad = input_gradient(cotangent, grad_pad, kernels[1])
-    minor_sums = lax.psum((minor_grads[0], minor_grads[1], minor_grads[2]), ("dp", "row", "col"))
+    minor_sums = lax.psum(
+        lax.psum((minor_grads[0], minor_grads[1], minor_grads[2]), ("row", "col")), "dp"
+    )
     owned = (
         lax.psum_scatter(large_grads[0], "dp", scatter_dimension=1, tiled=True),
         lax.psum_scatter(large_grads[1], "dp", scatter_dimension=0, tiled=True),

time: 831 us -> 736 us (0.89)
  waiting for transfers between devices: 470 us -> 382 us
  blocking collectives: 171 us -> 162 us
    reduce_scatter x1, waiting for transfers between devices: 79.1 us -> 0.02 us  [on_device(): lax.psum_scatter(large_grads[2], 'dp', scatter_dimension=0, tiled=True)]
    psum x1, blocking collectives: 77.7 us -> 17.5 us  [on_device(): lax.psum(lax.psum((minor_grads[0], minor_grads[1], minor_grads[2]), ('row...]
    psum x1, blocking collectives: 54.5 us -> 106 us  [on_device(): shares = lax.psum((owned[0], owned[1], owned[2]), ('row', 'col'))]
    reduce_scatter x1, waiting for transfers between devices: 85.7 us -> 54.2 us  [on_device(): lax.psum_scatter(large_grads[0], 'dp', scatter_dimension=1, tiled=True)]
    psum x1, waiting for transfers between devices: 56.6 us -> 78.8 us  [on_device(): lax.psum(lax.psum((minor_grads[0], minor_grads[1], minor_grads[2]), ('row...]
  transfers between devices with their start and end apart: 18 -> 18, of which waited for: 5 -> 4; matrix products, arithmetic and copies ran while one was open for 12% -> 17% of each run, Pallas kernels for 0% -> 0%
where the time goes in v1:
time: 736 us; the launch traced here: 731 us
  waiting for transfers between devices  382 us (52%)
  blocking collectives  162 us (22%)
  other arithmetic  91.7 us (12%)
  matrix products  33.4 us (5%)
  starting transfers between devices  32.8 us (4%)
  between operations  17.2 us (2%)
  local copies, waits for them, and re-layouts  11.8 us (2%)
    psum x1, waiting for transfers between devices, on_device(): shares = lax.psum((owned[0], owned[1], owned[2]), ('row', 'col'))  215 us
    psum x1, blocking collectives, on_device(): shares = lax.psum((owned[0], owned[1], owned[2]), ('row', 'col'))  106 us
    psum x1, waiting for transfers between devices, on_device(): lax.psum(lax.psum((minor_grads[0], minor_grads[1], minor_grads[2]), ('row...  78.8 us
    reduce_scatter x1, waiting for transfers between devices, on_device(): lax.psum_scatter(large_grads[0], 'dp', scatter_dimension=1, tiled=True)  54.2 us
    all_gather x1, waiting for transfers between devices, on_device(): lax.all_gather(weight_out, 'dp', axis=1, tiled=True)  32.6 us
    reduce_sum x2, other arithmetic, forward(): centered = convolved - jnp.mean(convolved, axis=-1, keepdims=True)  31.5 us
    ppermute x6, starting transfers between devices, with_halo(): before = lax.ppermute(last, axis, up)  22.1 us
    all_gather x1, blocking collectives, on_device(): lax.all_gather(bias_in, 'dp', axis=1, tiled=True)  19.5 us
  transfers between devices with their start and end apart: 18, of which 4 were waited for; matrix products, arithmetic and copies ran while one was open for 17% of the time, Pallas kernels for 0%

profile of v1, /device:TPU:1, one launch (start us, length us, event | category | flops | bytes accessed | tf_op | source)
XLA Modules:
  0.0 731.1 jit_solution(2152991851782614525)
XLA Ops:
  8.9 4.6 collective-permute-start
  13.5 1.9 collective-permute-start.1
  16.4 3.6 collective-permute-start.4
  20.0 1.9 collective-permute-start.5
  25.0 1.0 convert_reduce_fusion.54
  26.1 1.6 convert_reduce_fusion.55
  27.8 1.4 convert_reduce_fusion.3
  29.2 1.4 convert_reduce_fusion.56
  30.6 19.5 %all-gather = bf16[8,192,2]{1,2,0:T(2,128)(2,1)S(1)} all-gather(bf16[1,192,2]{1,2,0:T(2,128)(2,1)S(1)} %bitcast.59), channel_id=1, replica_groups=mesh['dp'=8,'row'=4,'col'=8] {'dp'}, dimensions={0}, use_global_device_ids=true | all-gather | bytes 6912 | tf_op jit(solution)/shard_map/all_gather | solution.py:126
  53.4 3.5 collective-permute-start.2
  56.9 1.3 collective-permute-start.3
  58.8 4.2 collective-permute-start.6
  63.0 1.5 collective-permute-start.7
  64.5 15.8 %fusion.250 = (f32[32,32]{1,0:T(8,128)S(1)}, f32[1,32,32,384]{3,2,1,0:T(8,128)S(1)}) fusion(f32[384]{0:T(512)S(1)} %get-tuple-element.174, f32[384]{0:T(512)S(1)} %get-tuple-element.117, bf16[1,38,3,384]{3,2,1,0:T(4,128)(2,1)S(1)} %collective-permute-done.3, bf16[1,38,32,384]{3,2,1,0:T(8,128)(2,1)S(1)} %get-tuple-element.222, ...), kind=kLoop, calls=%fused_computation.649 | loop fusion | flops 107740160 | bytes 8267776 | tf_op jit(solution)/shard_map/reduce_sum | solution.py:48
  81.3 15.7 %fusion.248 = (f32[32,32]{1,0:T(8,128)S(1)}, f32[1,32,32,384]{3,2,1,0:T(8,128)S(1)}) fusion(f32[384]{0:T(512)S(1)} %copy-done.111, f32[384]{0:T(512)S(1)} %get-tuple-element.146, bf16[1,38,3,384]{3,2,1,0:T(4,128)(2,1)S(1)} %collective-permute-done.7, bf16[1,38,32,384]{3,2,1,0:T(8,128)(2,1)S(1)} %get-tuple-element.218, f32[384]{0:T(512)S(1)} %get-tuple-element.127, ...), kind=kLoop, calls=%fused_computation.648 | loop fusion | flops 107740160 | bytes 8267776 | tf_op jit(solution)/shard_map/reduce_sum | solution.py:48
  97.7 1.5 add_convert_fusion
  99.2 6.7 multiply_convert_fusion
  105.9 32.6 %all-gather.6.cloned.1.call-done = bf16[2,1536,384]{2,1,0:T(8,128)(2,1)} async-done(((bf16[2,192,384]{2,1,0:T(8,128)(2,1)}), bf16[2,1536,384]{2,1,0:T(8,128)(2,1)}) %all-gather.6.cloned.1.call-update) | async-done | bytes 2359312 | tf_op jit(solution)/shard_map/all_gather | solution.py:127
  138.5 5.6 fusion.153
  144.1 3.3 fusion.258
  147.7 6.2 fusion.4
  154.0 2.9 fusion.247
  157.0 2.8 multiply_reduce_fusion
  161.8 4.2 fusion.149
  166.9 4.3 collective-permute-start.8
  171.2 2.1 collective-permute-start.9
  173.8 19.4 %all-reduce = f32[1536]{0:T(1024)S(1)} all-reduce(f32[1536]{0:T(1024)S(1)} %convert_reduce_fusion.1), channel_id=3, replica_groups=mesh['dp'=8,'row'=4,'col'=8] {'dp'}, use_global_device_ids=true, to_apply=%region_9.0.clone | all-reduce | flops 1536 | bytes 12288
  193.3 106.0 %all-reduce.1 = (f32[192]{0:T(256)}, f32[2,384]{1,0:T(2,128)S(1)}, f32[3,384]{1,0:T(4,128)S(1)}) all-reduce(f32[192]{0:T(256)S(1)} %dynamic-slice.1, f32[2,384]{1,0:T(2,128)S(1)} %pad_maximum_fusion.11, f32[3,384]{1,0:T(4,128)S(1)} %pad_maximum_fusion.10), channel_id=1, replica_groups=mesh['dp'=8,'row'=4,'col'=8] {'row','col'}, use_global_device_ids=true, to_apply=%region_10.0 | all-reduce | flops 2112 | bytes 16896 | tf_op jit(solution)/shard_map/psum | solution.py:164
  299.4 17.5 %all-reduce.3 = (f32[2,384]{1,0:T(2,128)}, f32[3,384]{1,0:T(4,128)S(1)}) all-reduce(f32[2,384]{1,0:T(2,128)S(1)} %get-tuple-element.181, f32[3,384]{1,0:T(4,128)S(1)} %get-tuple-element.182), channel_id=1, replica_groups=mesh['dp'=8,'row'=4,'col'=8] {'dp'}, use_global_device_ids=true, to_apply=%region_67.0 | all-reduce | flops 1920 | bytes 15360 | tf_op jit(solution)/shard_map/psum | solution.py:156
  317.5 1.0 fusion.148
  319.4 3.3 fusion.257
  323.0 5.5 convolution_add_fusion.1
  328.5 2.1 convert_add_fusion.1
  330.6 2.7 fusion.147
  333.3 3.1 fusion.151
  336.4 2.7 fusion.146
  339.2 3.2 fusion.150
  343.1 1.9 collective-permute-start.10
  345.1 1.3 collective-permute-start.11
  347.6 4.4 stack.220
  352.3 1.7 maximum_maximum_fusion
  354.0 54.2 %reduce-scatter.3.cloned.1.call-done = f32[384,192]{0,1:T(8,128)} async-done(((f32[384,1536]{0,1:T(8,128)}), f32[384,192]{0,1:T(8,128)}) %reduce-scatter.3.cloned.1.call-update) | async-done | bytes 294928 | tf_op jit(solution)/shard_map/reduce_scatter | solution.py:160
  408.6 16.6 %convert_add_fusion.2 = f32[1,32,32,384]{3,2,1,0:T(8,128)} fusion(bf16[1,32,32,384]{3,2,1,0:T(8,128)(2,1)} %param.11, bf16[1,32,32,384]{3,2,1,0:T(8,128)(2,1)S(1)} %multiply_convert_fusion.2, bf16[1,3,32,384]{3,2,1,0:T(8,128)(2,1)S(1)} %collective-permute-done.9, bf16[1,3,32,384]{3,2,1,0:T(8,128)(2,1)S(1)} %collective-permute-done.8, ...), kind=kLoop, calls=%fused_computation.342 | loop fusion | flops 60555264 | bytes 36398592 | tf_op jit(solution)/shard_map/add | solution.py:117
  425.3 215.2 %all-reduce.9.cloned.1.call-done = (f32[384,192]{0,1:T(8,128)}, f32[192,384]{1,0:T(8,128)}, f32[49,384]{1,0:T(8,128)}) async-done(((f32[384,192]{0,1:T(8,128)}, f32[192,384]{1,0:T(8,128)}, f32[49,384]{1,0:T(8,128)}), (f32[384,192]{0,1:T(8,128)}, f32[192,384]{1,0:T(8,128)}, f32[49,384]{1,0:T(8,128)})) %all-reduce.9.cloned.1.call-update) | async-done | bytes 665104 | tf_op jit(solution)/shard_map/psum | solution.py:164
  640.5 1.7 broadcast_multiply_fusion
  642.2 1.7 broadcast_multiply_fusion.1
  643.9 78.8 %all-reduce.7.cloned.1.call-done = f32[49,384]{1,0:T(8,128)} async-done(((f32[49,384]{1,0:T(8,128)}), f32[49,384]{1,0:T(8,128)}) %all-reduce.7.cloned.1.call-update) | async-done | bytes 75280 | tf_op jit(solution)/shard_map/psum | solution.py:156
  722.7 1.5 broadcast_multiply_fusion.2
  (364 shorter events, 17.3 us)
Async XLA Ops:
  7.2 92.0 %all-gather.4.cloned.1.call-start = ((), (), s32[]{:S(2)}) async-start(), calls=%async_computation.2 | async-start | bytes 2654208 | tf_op jit(solution)/shard_map/all_gather | solution.py:125
  7.9 130.6 %all-gather.6.cloned.1.call-start = ((), (), s32[]{:S(2)}) async-start(), calls=%async_computation.3 | async-start | bytes 2654208 | tf_op jit(solution)/shard_map/all_gather | solution.py:127
  8.9 43.8 %collective-permute-start = (bf16[1,3,32,384]{3,2,1,0:T(8,128)(2,1)S(1)}, bf16[1,3,32,384]{3,2,1,0:T(8,128)(2,1)S(1)}, u32[]{:S(2)}, u32[]{:S(2)}) collective-permute-start(bf16[1,3,32,384]{3,2,1,0:T(8,128)(2,1)S(1)} %get-tuple-element.214), channel_id=1, source_target_pairs={{0,8},{8,16},{16,24},{1,9},{9,17},{17,25},{2,10},{10,18},{18,26},{... | collective-permute-start | bytes 221192 | tf_op jit(solution)/shard_map/ppermute | solution.py:19
  13.5 39.7 %collective-permute-start.1 = (bf16[1,3,32,384]{3,2,1,0:T(8,128)(2,1)S(1)}, bf16[1,3,32,384]{3,2,1,0:T(8,128)(2,1)S(1)}, u32[]{:S(2)}, u32[]{:S(2)}) collective-permute-start(bf16[1,3,32,384]{3,2,1,0:T(8,128)(2,1)S(1)} %get-tuple-element.213), channel_id=1, source_target_pairs={{8,0},{16,8},{24,16},{9,1},{17,9},{25,17},{10,2},{18,10},{26,18},{... | collective-permute-start | bytes 221192 | tf_op jit(solution)/shard_map/ppermute | solution.py:20
  16.4 41.8 %collective-permute-start.4 = (bf16[1,3,32,384]{3,2,1,0:T(8,128)(2,1)S(1)}, bf16[1,3,32,384]{3,2,1,0:T(8,128)(2,1)S(1)}, u32[]{:S(2)}, u32[]{:S(2)}) collective-permute-start(bf16[1,3,32,384]{3,2,1,0:T(8,128)(2,1)S(1)} %get-tuple-element.209), channel_id=1, source_target_pairs={{0,8},{8,16},{16,24},{1,9},{9,17},{17,25},{2,10},{10,18},{18,26},{... | collective-permute-start | bytes 221192 | tf_op jit(solution)/shard_map/ppermute | solution.py:19
  20.0 38.6 %collective-permute-start.5 = (bf16[1,3,32,384]{3,2,1,0:T(8,128)(2,1)S(1)}, bf16[1,3,32,384]{3,2,1,0:T(8,128)(2,1)S(1)}, u32[]{:S(2)}, u32[]{:S(2)}) collective-permute-start(bf16[1,3,32,384]{3,2,1,0:T(8,128)(2,1)S(1)} %get-tuple-element.208), channel_id=1, source_target_pairs={{8,0},{16,8},{24,16},{9,1},{17,9},{25,17},{10,2},{18,10},{26,18},{... | collective-permute-start | bytes 221192 | tf_op jit(solution)/shard_map/ppermute | solution.py:20
  22.0 332.0 %reduce-scatter.5.cloned.1.call-start = ((), (), s32[]{:S(2)}) async-start(), calls=%async_computation.5 | async-start | bytes 2654208 | tf_op jit(solution)/shard_map/reduce_scatter | solution.py:162
  23.0 57.8 %copy-start.19 = (f32[384]{0:T(512)}, f32[384]{0:T(512)S(1)}, u32[]{:S(2)}) copy-start(f32[384]{0:T(512)S(1)} %get-tuple-element.114) | copy-start | bytes 4612
  23.0 57.8 %copy-start.21 = (f32[384]{0:T(512)}, f32[384]{0:T(512)S(1)}, u32[]{:S(2)}) copy-start(f32[384]{0:T(512)S(1)} %get-tuple-element.115) | copy-start | bytes 4612
  23.0 57.8 %copy-start.23 = (f32[384]{0:T(512)}, f32[384]{0:T(512)S(1)}, u32[]{:S(2)}) copy-start(f32[384]{0:T(512)S(1)} %get-tuple-element.116) | copy-start | bytes 4612
  24.0 56.8 %copy-start.25 = (f32[384]{0:T(512)}, f32[384]{0:T(512)S(1)}, u32[]{:S(2)}) copy-start(f32[384]{0:T(512)S(1)} %get-tuple-element.127) | copy-start | bytes 4612
  53.4 11.1 %collective-permute-start.2 = (bf16[1,38,3,384]{3,2,1,0:T(4,128)(2,1)S(1)}, bf16[1,38,3,384]{3,2,1,0:T(4,128)(2,1)S(1)}, u32[]{:S(2)}, u32[]{:S(2)}) collective-permute-start(bf16[1,38,3,384]{3,2,1,0:T(4,128)(2,1)S(1)} %get-tuple-element.198), channel_id=1, source_target_pairs={{0,1},{1,2},{2,3},{3,4},{4,5},{5,6},{6,7},{8,9},{9,10},{10,11},{11... | collective-permute-start | bytes 262664 | tf_op jit(solution)/shard_map/ppermute | solution.py:19
  56.9 7.6 %collective-permute-start.3 = (bf16[1,38,3,384]{3,2,1,0:T(4,128)(2,1)S(1)}, bf16[1,38,3,384]{3,2,1,0:T(4,128)(2,1)S(1)}, u32[]{:S(2)}, u32[]{:S(2)}) collective-permute-start(bf16[1,38,3,384]{3,2,1,0:T(4,128)(2,1)S(1)} %get-tuple-element.199), channel_id=1, source_target_pairs={{1,0},{2,1},{3,2},{4,3},{5,4},{6,5},{7,6},{9,8},{10,9},{11,10},{12... | collective-permute-start | bytes 262664 | tf_op jit(solution)/shard_map/ppermute | solution.py:20
  58.8 21.9 %collective-permute-start.6 = (bf16[1,38,3,384]{3,2,1,0:T(4,128)(2,1)S(1)}, bf16[1,38,3,384]{3,2,1,0:T(4,128)(2,1)S(1)}, u32[]{:S(2)}, u32[]{:S(2)}) collective-permute-start(bf16[1,38,3,384]{3,2,1,0:T(4,128)(2,1)S(1)} %get-tuple-element.196), channel_id=1, source_target_pairs={{0,1},{1,2},{2,3},{3,4},{4,5},{5,6},{6,7},{8,9},{9,10},{10,11},{11... | collective-permute-start | bytes 262664 | tf_op jit(solution)/shard_map/ppermute | solution.py:19
  63.0 17.8 %collective-permute-start.7 = (bf16[1,38,3,384]{3,2,1,0:T(4,128)(2,1)S(1)}, bf16[1,38,3,384]{3,2,1,0:T(4,128)(2,1)S(1)}, u32[]{:S(2)}, u32[]{:S(2)}) collective-permute-start(bf16[1,38,3,384]{3,2,1,0:T(4,128)(2,1)S(1)} %get-tuple-element.197), channel_id=1, source_target_pairs={{1,0},{2,1},{3,2},{4,3},{5,4},{6,5},{7,6},{9,8},{10,9},{11,10},{12... | collective-permute-start | bytes 262664 | tf_op jit(solution)/shard_map/ppermute | solution.py:20
  147.4 260.8 %reduce-scatter.3.cloned.1.call-start = ((), (), s32[]{:S(2)}) async-start(), calls=%async_computation.4 | async-start | bytes 2654208 | tf_op jit(solution)/shard_map/reduce_scatter | solution.py:160
  166.9 176.1 %collective-permute-start.8 = (bf16[1,3,32,384]{3,2,1,0:T(8,128)(2,1)}, bf16[1,3,32,384]{3,2,1,0:T(8,128)(2,1)S(1)}, u32[]{:S(2)}, u32[]{:S(2)}) collective-permute-start(bf16[1,3,32,384]{3,2,1,0:T(8,128)(2,1)} %get-tuple-element.203), channel_id=1, source_target_pairs={{0,8},{8,16},{16,24},{1,9},{9,17},{17,25},{2,10},{10,18},{18,26},{... | collective-permute-start | bytes 221192 | tf_op jit(solution)/shard_map/ppermute | solution.py:19
  171.2 146.3 %copy-start.4 = (bf16[1,35,32,384]{3,2,1,0:T(8,128)(2,1)S(1)}, bf16[1,35,32,384]{3,2,1,0:T(8,128)(2,1)}, u32[]{:S(2)}) copy-start(bf16[1,35,32,384]{3,2,1,0:T(8,128)(2,1)} %copy-done.3) | copy-start | bytes 2580484
  171.2 171.8 %collective-permute-start.9 = (bf16[1,3,32,384]{3,2,1,0:T(8,128)(2,1)}, bf16[1,3,32,384]{3,2,1,0:T(8,128)(2,1)S(1)}, u32[]{:S(2)}, u32[]{:S(2)}) collective-permute-start(bf16[1,3,32,384]{3,2,1,0:T(8,128)(2,1)} %get-tuple-element.204), channel_id=1, source_target_pairs={{8,0},{16,8},{24,16},{9,1},{17,9},{25,17},{10,2},{18,10},{26,18},{... | collective-permute-start | bytes 221192 | tf_op jit(solution)/shard_map/ppermute | solution.py:20
  173.3 145.2 %copy-start.16 = (bf16[1,32,32,384]{3,2,1,0:T(8,128)(2,1)S(1)}, bf16[1,32,32,384]{3,2,1,0:T(8,128)(2,1)}, u32[]{:S(2)}) copy-start(bf16[1,32,32,384]{3,2,1,0:T(8,128)(2,1)} %copy-done.15) | copy-start | bytes 2359300
  322.7 317.8 %all-reduce.9.cloned.1.call-start = ((), (), s32[]{:S(2)}) async-start(), calls=%async_computation.7 | async-start | bytes 1351680 | tf_op jit(solution)/shard_map/psum | solution.py:164
  343.1 8.8 %collective-permute-start.10 = (bf16[1,38,3,384]{3,2,1,0:T(4,128)(2,1)S(1)}, bf16[1,38,3,384]{3,2,1,0:T(4,128)(2,1)}, u32[]{:S(2)}, u32[]{:S(2)}) collective-permute-start(bf16[1,38,3,384]{3,2,1,0:T(4,128)(2,1)S(1)} %get-tuple-element.194), channel_id=1, source_target_pairs={{0,1},{1,2},{2,3},{3,4},{4,5},{5,6},{6,7},{8,9},{9,10},{10,11},{11... | collective-permute-start | bytes 262664 | tf_op jit(solution)/shard_map/ppermute | solution.py:19
  345.1 7.2 collective-permute-start.11
  351.9 56.4 %copy-start.26 = (f32[384]{0:T(512)S(1)}, f32[384]{0:T(512)}, u32[]{:S(2)}) copy-start(f32[384]{0:T(512)} %copy-done.25) | copy-start | bytes 4612
  351.9 56.4 %copy-start.28 = (f32[384]{0:T(512)S(1)}, f32[384]{0:T(512)}, u32[]{:S(2)}) copy-start(f32[384]{0:T(512)} %copy-done.27) | copy-start | bytes 4612
  351.9 56.4 %copy-start.30 = (f32[384]{0:T(512)S(1)}, f32[384]{0:T(512)}, u32[]{:S(2)}) copy-start(f32[384]{0:T(512)} %copy-done.29) | copy-start | bytes 4612
  352.0 56.4 %copy-start.32 = (f32[384]{0:T(512)S(1)}, f32[384]{0:T(512)}, u32[]{:S(2)}) copy-start(f32[384]{0:T(512)} %copy-done.31) | copy-start | bytes 4612
  352.0 56.4 %copy-start.34 = (f32[384]{0:T(512)S(1)}, f32[384]{0:T(512)}, u32[]{:S(2)}) copy-start(f32[384]{0:T(512)} %copy-done.33) | copy-start | bytes 4612
  352.0 56.4 %copy-start.36 = (f32[384]{0:T(512)S(1)}, f32[384]{0:T(512)}, u32[]{:S(2)}) copy-start(f32[384]{0:T(512)} %copy-done.35) | copy-start | bytes 4612
  352.0 56.4 %copy-start.38 = (f32[384]{0:T(512)S(1)}, f32[384]{0:T(512)}, u32[]{:S(2)}) copy-start(f32[384]{0:T(512)} %copy-done.37) | copy-start | bytes 4612
  352.0 56.4 %copy-start.40 = (f32[384]{0:T(512)S(1)}, f32[384]{0:T(512)}, u32[]{:S(2)}) copy-start(f32[384]{0:T(512)} %copy-done.39) | copy-start | bytes 4612
  352.0 56.4 %copy-start.42 = (f32[384]{0:T(512)S(1)}, f32[384]{0:T(512)}, u32[]{:S(2)}) copy-start(f32[384]{0:T(512)} %copy-done.41) | copy-start | bytes 4612
  352.0 56.4 %copy-start.44 = (f32[384]{0:T(512)S(1)}, f32[384]{0:T(512)}, u32[]{:S(2)}) copy-start(f32[384]{0:T(512)} %copy-done.43) | copy-start | bytes 4612
  352.0 56.4 %copy-start.46 = (f32[384]{0:T(512)S(1)}, f32[384]{0:T(512)}, u32[]{:S(2)}) copy-start(f32[384]{0:T(512)} %copy-done.45) | copy-start | bytes 4612
  352.0 56.4 %copy-start.48 = (f32[384]{0:T(512)S(1)}, f32[384]{0:T(512)}, u32[]{:S(2)}) copy-start(f32[384]{0:T(512)} %copy-done.47) | copy-start | bytes 4612
  352.1 56.4 %copy-start.50 = (f32[384]{0:T(512)S(1)}, f32[384]{0:T(512)}, u32[]{:S(2)}) copy-start(f32[384]{0:T(512)} %copy-done.49) | copy-start | bytes 4612
  352.1 56.4 %copy-start.52 = (f32[384]{0:T(512)S(1)}, f32[384]{0:T(512)}, u32[]{:S(2)}) copy-start(f32[384]{0:T(512)} %copy-done.51) | copy-start | bytes 4612
  352.1 56.4 %copy-start.54 = (f32[384]{0:T(512)S(1)}, f32[384]{0:T(512)}, u32[]{:S(2)}) copy-start(f32[384]{0:T(512)} %copy-done.53) | copy-start | bytes 4612
  352.1 56.4 %copy-start.56 = (f32[384]{0:T(512)S(1)}, f32[384]{0:T(512)}, u32[]{:S(2)}) copy-start(f32[384]{0:T(512)} %copy-done.55) | copy-start | bytes 4612
  352.1 56.4 %copy-start.58 = (f32[384]{0:T(512)S(1)}, f32[384]{0:T(512)}, u32[]{:S(2)}) copy-start(f32[384]{0:T(512)} %copy-done.57) | copy-start | bytes 4612
  352.1 56.4 %copy-start.60 = (f32[384]{0:T(512)S(1)}, f32[384]{0:T(512)}, u32[]{:S(2)}) copy-start(f32[384]{0:T(512)} %copy-done.59) | copy-start | bytes 4612
  352.1 56.4 %copy-start.62 = (f32[384]{0:T(512)S(1)}, f32[384]{0:T(512)}, u32[]{:S(2)}) copy-start(f32[384]{0:T(512)} %copy-done.61) | copy-start | bytes 4612
  352.1 56.4 %copy-start.64 = (f32[384]{0:T(512)S(1)}, f32[384]{0:T(512)}, u32[]{:S(2)}) copy-start(f32[384]{0:T(512)} %copy-done.63) | copy-start | bytes 4612
  352.1 56.4 %copy-start.66 = (f32[384]{0:T(512)S(1)}, f32[384]{0:T(512)}, u32[]{:S(2)}) copy-start(f32[384]{0:T(512)} %copy-done.65) | copy-start | bytes 4612
  352.1 56.4 %copy-start.68 = (f32[384]{0:T(512)S(1)}, f32[384]{0:T(512)}, u32[]{:S(2)}) copy-start(f32[384]{0:T(512)} %copy-done.67) | copy-start | bytes 4612
  352.2 56.4 %copy-start.70 = (f32[384]{0:T(512)S(1)}, f32[384]{0:T(512)}, u32[]{:S(2)}) copy-start(f32[384]{0:T(512)} %copy-done.69) | copy-start | bytes 4612
  352.2 56.4 %copy-start.72 = (f32[384]{0:T(512)S(1)}, f32[384]{0:T(512)}, u32[]{:S(2)}) copy-start(f32[384]{0:T(512)} %copy-done.71) | copy-start | bytes 4612
  408.2 314.4 %all-reduce.7.cloned.1.call-start = ((), (), s32[]{:S(2)}) async-start(), calls=%async_computation.6 | async-start | bytes 172032 | tf_op jit(solution)/shard_map/psum | solution.py:156
  (93 other events, 2760.7 us)
Sparse Core Ops, SparseCore 0:
  10.6 64.3 all-gather.3
  77.6 60.8 all-gather.5
  147.5 81.9 reduce-scatter.4
  322.8 85.3 reduce-scatter.2
  411.5 228.9 all-reduce.8
  643.0 79.6 all-reduce.6
